TPU v7x, 32 devices: a whole 2x2x4 slice. The times are simulated.
32 devices in a mesh: vocab: 8 (over z, x), batch: 4 (over y, core).
Axes of the slice: x: 2, y: 2, z: 4, core: 2. Of those that a mesh axis runs over, the one named last changes fastest.
Arguments:
- hidden: bfloat16 [256, 1024], P(('vocab', 'batch'))
- embedding: bfloat16 [8192, 1024], P('vocab')
- block_counts: int32 [64], P('vocab'), may hold values from 1 to 4095
- lang_blocks: int32 [200, 64], replicated, may hold values from -1 to 63, as said below
- sent_lang: int32 [4], replicated, may hold values from 0 to 199
- targets: int32 [256], replicated, may hold values from 0 to 8191, as said below
Outputs:
- token_loss: float32 [256], P(('vocab', 'batch'))
- grad_embed: bfloat16 [8192, 1024], P(('vocab', 'batch'))
Inputs may be any that keep to these rules, and one draw needn't show every extreme that they name: `lang_blocks`: each list holds distinct block numbers and then -1 padding; the first entry of every list is block 0; at least 16 entries are blocks, and some language fills all 64 entries. `targets`: the target of token t lies in a block listed for the language of sentence t // 64.
All inputs are finite; a program needn't handle non-finite values.
Results may differ from a plain program's by a relative error of at most 0.0075.
Values may be sent and summed in bfloat16 or wider, within the bound.
No kernel may reach another device: no remote copies, remote signals or barrier semaphores. Data moves between devices by JAX's collectives and lax.ppermute only.
A program may use at most 64 MiB of HBM per device.

v0:
```python
import jax
import jax.numpy as jnp
from jax import lax
from jax.sharding import PartitionSpec as P

SEQ = 64
masked_fill = -1e30


def body(hidden, embedding, block_counts, lang_blocks, sent_lang, targets):
    tok_dev = hidden.shape[0]
    vocab_count = lax.axis_size("vocab")
    batch_count = lax.axis_size("batch")
    vocab_index = lax.axis_index("vocab")
    batch_index = lax.axis_index("batch")
    local_rows = embedding.shape[0]
    local_blocks = block_counts.shape[0]
    block_width = local_rows // local_blocks
    gathered = lax.all_gather(hidden, "vocab", axis=0, tiled=True)
    token_count = gathered.shape[0]
    token_ids = (
        (jnp.arange(vocab_count, dtype=jnp.int32)[:, None] * batch_count + batch_index) * tok_dev
        + jnp.arange(tok_dev, dtype=jnp.int32)[None, :]
    ).reshape(-1)
    target_ids = lax.dynamic_index_in_dim(
        targets.reshape(vocab_count, batch_count, tok_dev), batch_index, 1, keepdims=False
    ).reshape(-1)
    sentence = token_ids // SEQ
    sentence_hit = sentence[:, None] == jnp.arange(sent_lang.shape[0], dtype=jnp.int32)[None, :]
    token_language = jnp.sum(jnp.where(sentence_hit, sent_lang[None, :], 0), axis=1)
    block_ids = vocab_index * local_blocks + jnp.arange(local_blocks, dtype=jnp.int32)
    member = jnp.any(lang_blocks[:, :, None] == block_ids[None, None, :], axis=1).astype(
        jnp.float32
    )
    language_hit = (
        token_language[:, None] == jnp.arange(lang_blocks.shape[0], dtype=jnp.int32)[None, :]
    ).astype(jnp.float32)
    allowed = jnp.dot(language_hit, member, precision=lax.Precision.HIGHEST) > 0.5
    allowed_cells = allowed[:, :, None]
    raw_scores = lax.dot_general(
        gathered, embedding, (((1,), (1,)), ((), ())), preferred_element_type=jnp.float32
    )
    log_sampling = jnp.log(block_counts.astype(jnp.float32))
    logits = (
        raw_scores.reshape(token_count, local_blocks, block_width) - log_sampling[None, :, None]
    )
    masked = jnp.where(allowed_cells, logits, masked_fill)
    word_ids = (vocab_index * local_rows + jnp.arange(local_rows, dtype=jnp.int32)).reshape(
        local_blocks, block_width
    )
    is_target = word_ids[None, :, :] == target_ids[:, None, None]
    local_peak = jnp.max(masked, axis=(1, 2))
    local_target = jnp.sum(jnp.where(is_target, logits, 0.0), axis=(1, 2))
    peak_value = lax.pmax(local_peak, "vocab")
    local_total = jnp.sum(
        jnp.where(allowed_cells, jnp.exp(masked - peak_value[:, None, None]), 0.0), axis=(1, 2)
    )
    denominator, target_logit = lax.psum((local_total, local_target), "vocab")
    log_total = peak_value + jnp.log(denominator)
    every_loss = log_total - target_logit
    token_loss = lax.dynamic_slice_in_dim(every_loss, vocab_index * tok_dev, tok_dev, 0)
    softmax_weights = jnp.where(allowed_cells, jnp.exp(logits - log_total[:, None, None]), 0.0)
    grad_logits = (
        (softmax_weights - is_target.astype(jnp.float32))
        .astype(jnp.bfloat16)
        .reshape(token_count, local_rows)
    )
    columns = lax.all_to_all(grad_logits, "batch", split_axis=1, concat_axis=0, tiled=True)
    everyone = lax.all_gather(gathered, "batch", axis=0, tiled=True)
    summed = jnp.zeros((columns.shape[1], gathered.shape[1]), jnp.float32)
    for source in range(batch_count):
        slice_grad = columns[source * token_count : (source + 1) * token_count]
        slice_rows = everyone[source * token_count : (source + 1) * token_count]
        contribution = lax.dot_general(
            slice_grad, slice_rows, (((0,), (0,)), ((), ())), preferred_element_type=jnp.float32
        )
        rounded = lax.optimization_barrier(contribution.astype(jnp.bfloat16))
        summed = summed + rounded.astype(jnp.float32)
    grad_embed = summed.astype(jnp.bfloat16)
    return (token_loss, grad_embed)


def solution(mesh):
    in_specs = (P(("vocab", "batch"), None), P("vocab", None), P("vocab"), P(), P(), P())
    out_specs = (P(("vocab", "batch")), P(("vocab", "batch"), None))
    return jax.shard_map(body, mesh=mesh, in_specs=in_specs, out_specs=out_specs, check_vma=False)
```

profile of v0, /device:TPU:0, one launch (start us, length us, event | category | flops | bytes accessed | tf_op | source)
XLA Modules:
  0.0 92.3 jit_solution(3741572874803002125)
XLA Ops:
  0.6 0.0 copy-start
  0.7 0.8 convert_log_fusion
  1.5 0.1 broadcast_bitcast_fusion
  1.6 0.1 iota_add_fusion
  1.6 0.1 add.93
  1.7 1.0 %compare_reduce_fusion = pred[200,8]{0,1:T(8,128)(4,1)S(1)} fusion(s32[200,64]{0,1:T(8,128)} %param.9, s32[8]{0:T(128)S(1)} %iota_add_fusion.1), kind=kLoop, calls=%fused_computation.7 | loop fusion | flops 203200 | bytes 52832 | tf_op jit(solution)/shard_map/reduce_or | solution.py:32
  2.7 0.7 select_reduce_fusion.1
  3.5 0.2 convolution_compare_fusion
  3.7 0.1 copy.13
  3.8 0.8 reshape.91
  4.6 0.1 eq.66
  4.7 32.5 %all_gather.6 = bf16[64,1024]{1,0:T(8,128)(2,1)S(1)} all-gather(bf16[8,1024]{1,0:T(8,128)(2,1)} %param.6), channel_id=1, replica_groups=mesh['vocab'=8,'batch'=4] {'vocab'}, dimensions={0}, use_global_device_ids=true | all-gather | bytes 147456 | tf_op jit(solution)/shard_map/all_gather | solution.py:19
  37.2 0.1 broadcast_in_dim.53
  37.3 0.0 copy-done
  37.3 0.9 fusion.3
  38.2 21.3 %pmax.7 = f32[64]{0:T(128)S(1)} all-reduce(f32[64]{0:T(128)S(1)} %get-tuple-element.8), channel_id=1, replica_groups=mesh['vocab'=8,'batch'=4] {'vocab'}, use_global_device_ids=true, to_apply=%region_3.4 | all-reduce | flops 64 | bytes 512 | tf_op jit(solution)/shard_map/pmax | solution.py:54
  59.5 0.3 fusion
  59.8 17.1 %all-reduce = (f32[64]{0:T(128)S(1)}, f32[64]{0:T(128)S(1)}) all-reduce(f32[64]{0:T(128)S(1)} %get-tuple-element.3, f32[64]{0:T(128)S(1)} %get-tuple-element.2), channel_id=1, replica_groups=mesh['vocab'=8,'batch'=4] {'vocab'}, use_global_device_ids=true, to_apply=%region_5.6 | all-reduce | flops 128 | bytes 1024 | tf_op jit(solution)/shard_map/psum | solution.py:58
  76.9 0.1 fusion.2
  77.1 0.7 copy.21
  77.7 3.3 %all-to-all-start = ((bf16[64,4,256]{2,0,1:T(8,128)(2,1)}), bf16[64,4,256]{2,0,1:T(8,128)(2,1)S(1)}, u32[]{:S(2)}, u32[]{:S(2)}) async-start(bf16[64,4,256]{2,0,1:T(8,128)(2,1)} %bitcast.32), calls=%async_computation | async-start | bytes 262144 | tf_op jit(solution)/shard_map/all_to_all | solution.py:68
  81.1 8.2 %all_gather.7 = bf16[256,1024]{1,0:T(8,128)(2,1)S(1)} all-gather(bf16[64,1024]{1,0:T(8,128)(2,1)S(1)} %all_gather.6), channel_id=1, replica_groups=mesh['vocab'=8,'batch'=4] {'batch'}, dimensions={0}, use_global_device_ids=true | all-gather | bytes 655360 | tf_op jit(solution)/shard_map/all_gather | solution.py:69
  89.3 0.6 dynamic_slice.8
  89.9 0.0 all-to-all-done
  89.9 0.3 convolution_convert_fusion
  90.2 0.3 convolution_convert_fusion.1
  90.5 0.3 convolution_convert_fusion.2
  90.9 0.3 convolution_convert_fusion.3
  91.2 1.1 %add_convert_fusion = bf16[256,1024]{1,0:T(8,128)(2,1)} fusion(bf16[256,1024]{1,0:T(8,128)(2,1)S(1)} %convolution_convert_fusion, bf16[256,1024]{1,0:T(8,128)(2,1)S(1)} %convolution_convert_fusion.1, bf16[256,1024]{1,0:T(8,128)(2,1)S(1)} %convolution_convert_fusion.2, bf16[256,1024]{1,0:T(8,128)(2,1)S(1)} %convolution_convert_fusion.3), kind=kLoop, calls=%fused_computation.6 | loop fusion | flops 2097152 | bytes 2621440 | tf_op jit(solution)/shard_map/convert_element_type | solution.py:79
  (6 shorter events, 0.1 us)
Async XLA Ops:
  0.6 36.7 %copy-start = (bf16[1024,1024]{1,0:T(8,128)(2,1)S(1)}, bf16[1024,1024]{1,0:T(8,128)(2,1)}, u32[]{:S(2)}) copy-start(bf16[1024,1024]{1,0:T(8,128)(2,1)} %param.7) | copy-start | bytes 6291460
  77.7 12.2 %all-to-all-start = ((bf16[64,4,256]{2,0,1:T(8,128)(2,1)}), bf16[64,4,256]{2,0,1:T(8,128)(2,1)S(1)}, u32[]{:S(2)}, u32[]{:S(2)}) async-start(bf16[64,4,256]{2,0,1:T(8,128)(2,1)} %bitcast.32), calls=%async_computation | async-start | bytes 262144 | tf_op jit(solution)/shard_map/all_to_all | solution.py:68
where the time goes:
time: 92.7 us; the launch traced here: 92.3 us
  blocking collectives  79.2 us (85%)
  other arithmetic  4.2 us (5%)
  starting transfers between devices  3.33 us (4%)
  local copies, waits for them, and re-layouts  2.52 us (3%)
  matrix products  2.32 us (3%)
    all_gather x1, blocking collectives, body(): gathered = lax.all_gather(hidden, 'vocab', axis=0, tiled=True)  32.5 us
    pmax x1, blocking collectives, body(): peak_value = lax.pmax(local_peak, 'vocab')  21.3 us
    psum x1, blocking collectives, body(): denominator, target_logit = lax.psum((local_total, local_target), 'vocab')  17.1 us
    all_gather x1, blocking collectives, body(): everyone = lax.all_gather(gathered, 'batch', axis=0, tiled=True)  8.24 us
    all_to_all x1, starting transfers between devices, body(): lax.all_to_all(grad_logits, 'batch', split_axis=1, concat_axis=0, tiled=T...  3.33 us
  transfers between devices with their start and end apart: 1, of which 0 were waited for; matrix products, arithmetic and copies ran while one was open for 1% of the time, Pallas kernels for 0%

commit v1 on v0

--- a/solution.py
+++ b/solution.py
@@ -16,7 +16,16 @@
     local_rows = embedding.shape[0]
     local_blocks = block_counts.shape[0]
     block_width = local_rows // local_blocks
-    gathered = lax.all_gather(hidden, "vocab", axis=0, tiled=True)
+    size, here, width = (lax.axis_size("vocab"), lax.axis_index("vocab"), hidden.shape[0])
+    forward = [(i, (i + 1) % size) for i in range(size)]
+    out = jnp.zeros((*hidden.shape[:0], size * width, *hidden.shape[0 + 1 :]), hidden.dtype)
+    held = hidden
+    for step in range(size):
+        owner = (here - step) % size
+        out = lax.dynamic_update_slice_in_dim(out, held, owner * width, axis=0)
+        if step < size - 1:
+            held = lax.ppermute(held, "vocab", forward)
+    gathered = out
     token_count = gathered.shape[0]
     token_ids = (
         (jnp.arange(vocab_count, dtype=jnp.int32)[:, None] * batch_count + batch_index) * tok_dev

time: 92.7 us -> 101 us (1.090)
  waiting for transfers between devices: 0.01 us -> 37.8 us
  blocking collectives: 79.2 us -> 44.5 us
  starting transfers between devices: 3.33 us -> 7.58 us
    ppermute x0 -> x7, waiting for transfers between devices: none -> 37.8 us  [body(): held = lax.ppermute(held, 'vocab', forward)]
    all_gather x1 -> x0, blocking collectives: 32.5 us -> none  [body(): gathered = lax.all_gather(hidden, 'vocab', axis=0, tiled=True)]
    ppermute x0 -> x7, starting transfers between devices: none -> 4.26 us  [body(): held = lax.ppermute(held, 'vocab', forward)]
    pmax x1, blocking collectives: 21.3 us -> 17.1 us  [body(): peak_value = lax.pmax(local_peak, 'vocab')]
    psum x1, blocking collectives: 17.1 us -> 19.1 us  [body(): denominator, target_logit = lax.psum((local_total, local_target), 'vocab')]
  transfers between devices with their start and end apart: 1 -> 8, of which waited for: 0 -> 7; matrix products, arithmetic and copies ran while one was open for 1% -> 5% of each run, Pallas kernels for 0% -> 0%
where the time goes in v1:
time: 101 us; the launch traced here: 100 us
  blocking collectives  44.5 us (44%)
  waiting for transfers between devices  37.8 us (37%)
  starting transfers between devices  7.58 us (8%)
  other arithmetic  4.05 us (4%)
  local copies, waits for them, and re-layouts  3.27 us (3%)
  matrix products  2.31 us (2%)
    ppermute x7, waiting for transfers between devices, body(): held = lax.ppermute(held, 'vocab', forward)  37.8 us
    psum x1, blocking collectives, body(): denominator, target_logit = lax.psum((local_total, local_target), 'vocab')  19.1 us
    pmax x1, blocking collectives, body(): peak_value = lax.pmax(local_peak, 'vocab')  17.1 us
    all_gather x1, blocking collectives, body(): everyone = lax.all_gather(gathered, 'batch', axis=0, tiled=True)  8.24 us
    ppermute x7, starting transfers between devices, body(): held = lax.ppermute(held, 'vocab', forward)  4.26 us
    all_to_all x1, starting transfers between devices, body(): lax.all_to_all(grad_logits, 'batch', split_axis=1, concat_axis=0, tiled=T...  3.33 us
  transfers between devices with their start and end apart: 8, of which 7 were waited for; matrix products, arithmetic and copies ran while one was open for 5% of the time, Pallas kernels for 0%

profile of v1, /device:TPU:0, one launch (start us, length us, event | category | flops | bytes accessed | tf_op | source)
XLA Modules:
  0.0 100.3 jit_solution(8459681493124986939)
XLA Ops:
  0.6 0.0 copy-start
  0.6 3.0 %collective-permute-start = (bf16[8,1024]{1,0:T(8,128)(2,1)}, bf16[8,1024]{1,0:T(8,128)(2,1)S(1)}, u32[]{:S(2)}, u32[]{:S(2)}) collective-permute-start(bf16[8,1024]{1,0:T(8,128)(2,1)} %param.6), channel_id=1, source_target_pairs={{0,4},{4,8},{8,12},{12,16},{16,20},{20,24},{24,28},{28,0},{1,5},{5... | collective-permute-start | bytes 49160 | tf_op jit(solution)/shard_map/ppermute | solution.py:27
  3.7 0.7 convert_log_fusion
  4.3 0.1 broadcast_bitcast_fusion
  4.4 0.1 iota_add_fusion
  4.5 0.1 add.149
  4.6 1.0 compare_reduce_fusion
  5.6 0.7 select_reduce_fusion.1
  6.3 0.2 convolution_compare_fusion
  6.5 0.7 constant_dynamic-update-slice_fusion.7
  7.3 0.1 copy.13
  7.4 0.8 reshape.91
  8.2 0.1 eq.75
  8.3 0.4 collective-permute-done
  8.6 1.2 %collective-permute-start.1 = (bf16[8,1024]{1,0:T(8,128)(2,1)S(1)}, bf16[8,1024]{1,0:T(8,128)(2,1)S(1)}, u32[]{:S(2)}, u32[]{:S(2)}) collective-permute-start(bf16[8,1024]{1,0:T(8,128)(2,1)S(1)} %collective-permute-done), channel_id=1, source_target_pairs={{0,4},{4,8},{8,12},{12,16},{16,20},{20,24},{24,28},{28,0},{1,5},{5... | collective-permute-start | bytes 49160 | tf_op jit(solution)/shard_map/ppermute | solution.py:27
  9.9 5.2 %collective-permute-done.1 = bf16[8,1024]{1,0:T(8,128)(2,1)S(1)} collective-permute-done((bf16[8,1024]{1,0:T(8,128)(2,1)S(1)}, bf16[8,1024]{1,0:T(8,128)(2,1)S(1)}, u32[]{:S(2)}, u32[]{:S(2)}) %collective-permute-start.1) | collective-permute-done | bytes 16416 | tf_op jit(solution)/shard_map/ppermute | solution.py:27
  15.1 0.0 collective-permute-start.2
  15.1 6.4 %collective-permute-done.2 = bf16[8,1024]{1,0:T(8,128)(2,1)S(1)} collective-permute-done((bf16[8,1024]{1,0:T(8,128)(2,1)S(1)}, bf16[8,1024]{1,0:T(8,128)(2,1)S(1)}, u32[]{:S(2)}, u32[]{:S(2)}) %collective-permute-start.2) | collective-permute-done | bytes 16416 | tf_op jit(solution)/shard_map/ppermute | solution.py:27
  21.5 0.0 collective-permute-start.3
  21.5 6.4 %collective-permute-done.3 = bf16[8,1024]{1,0:T(8,128)(2,1)S(1)} collective-permute-done((bf16[8,1024]{1,0:T(8,128)(2,1)S(1)}, bf16[8,1024]{1,0:T(8,128)(2,1)S(1)}, u32[]{:S(2)}, u32[]{:S(2)}) %collective-permute-start.3) | collective-permute-done | bytes 16416 | tf_op jit(solution)/shard_map/ppermute | solution.py:27
  27.9 0.0 collective-permute-start.4
  27.9 6.5 %collective-permute-done.4 = bf16[8,1024]{1,0:T(8,128)(2,1)S(1)} collective-permute-done((bf16[8,1024]{1,0:T(8,128)(2,1)S(1)}, bf16[8,1024]{1,0:T(8,128)(2,1)S(1)}, u32[]{:S(2)}, u32[]{:S(2)}) %collective-permute-start.4) | collective-permute-done | bytes 16416 | tf_op jit(solution)/shard_map/ppermute | solution.py:27
  34.5 0.0 collective-permute-start.5
  34.5 6.4 %collective-permute-done.5 = bf16[8,1024]{1,0:T(8,128)(2,1)S(1)} collective-permute-done((bf16[8,1024]{1,0:T(8,128)(2,1)S(1)}, bf16[8,1024]{1,0:T(8,128)(2,1)S(1)}, u32[]{:S(2)}, u32[]{:S(2)}) %collective-permute-start.5) | collective-permute-done | bytes 16416 | tf_op jit(solution)/shard_map/ppermute | solution.py:27
  40.9 0.0 collective-permute-start.6
  40.9 6.4 %collective-permute-done.6 = bf16[8,1024]{1,0:T(8,128)(2,1)S(1)} collective-permute-done((bf16[8,1024]{1,0:T(8,128)(2,1)S(1)}, bf16[8,1024]{1,0:T(8,128)(2,1)S(1)}, u32[]{:S(2)}, u32[]{:S(2)}) %collective-permute-start.6) | collective-permute-done | bytes 16416 | tf_op jit(solution)/shard_map/ppermute | solution.py:27
  47.3 0.1 broadcast_in_dim.56
  47.5 0.0 copy-done
  47.5 0.9 fusion.3
  48.3 17.1 %pmax.7 = f32[64]{0:T(128)S(1)} all-reduce(f32[64]{0:T(128)S(1)} %get-tuple-element.8), channel_id=1, replica_groups=mesh['vocab'=8,'batch'=4] {'vocab'}, use_global_device_ids=true, to_apply=%region_3.4 | all-reduce | flops 64 | bytes 512 | tf_op jit(solution)/shard_map/pmax | solution.py:63
  65.5 0.3 fusion
  65.7 19.1 %all-reduce = (f32[64]{0:T(128)S(1)}, f32[64]{0:T(128)S(1)}) all-reduce(f32[64]{0:T(128)S(1)} %get-tuple-element.3, f32[64]{0:T(128)S(1)} %get-tuple-element.2), channel_id=1, replica_groups=mesh['vocab'=8,'batch'=4] {'vocab'}, use_global_device_ids=true, to_apply=%region_5.6 | all-reduce | flops 128 | bytes 1024 | tf_op jit(solution)/shard_map/psum | solution.py:67
  84.9 0.1 fusion.2
  85.0 0.7 copy.21
  85.7 3.3 %all-to-all-start = ((bf16[64,4,256]{2,0,1:T(8,128)(2,1)}), bf16[64,4,256]{2,0,1:T(8,128)(2,1)S(1)}, u32[]{:S(2)}, u32[]{:S(2)}) async-start(bf16[64,4,256]{2,0,1:T(8,128)(2,1)} %bitcast.32), calls=%async_computation | async-start | bytes 262144 | tf_op jit(solution)/shard_map/all_to_all | solution.py:77
  89.0 8.2 %all_gather.3 = bf16[256,1024]{1,0:T(8,128)(2,1)S(1)} all-gather(bf16[64,1024]{1,0:T(8,128)(2,1)S(1)} %constant_dynamic-update-slice_fusion), channel_id=1, replica_groups=mesh['vocab'=8,'batch'=4] {'batch'}, dimensions={0}, use_global_device_ids=true | all-gather | bytes 655360 | tf_op jit(solution)/shard_map/all_gather | solution.py:78
  97.3 0.6 dynamic_slice.8
  97.8 0.0 all-to-all-done
  97.8 0.3 convolution_convert_fusion
  98.2 0.3 convolution_convert_fusion.1
  98.5 0.3 convolution_convert_fusion.2
  98.8 0.3 convolution_convert_fusion.3
  99.1 1.1 %add_convert_fusion = bf16[256,1024]{1,0:T(8,128)(2,1)} fusion(bf16[256,1024]{1,0:T(8,128)(2,1)S(1)} %convolution_convert_fusion, bf16[256,1024]{1,0:T(8,128)(2,1)S(1)} %convolution_convert_fusion.1, bf16[256,1024]{1,0:T(8,128)(2,1)S(1)} %convolution_convert_fusion.2, bf16[256,1024]{1,0:T(8,128)(2,1)S(1)} %convolution_convert_fusion.3), kind=kLoop, calls=%fused_computation.6 | loop fusion | flops 2097152 | bytes 2621440 | tf_op jit(solution)/shard_map/convert_element_type | solution.py:88
  (14 shorter events, 0.1 us)
Async XLA Ops:
  0.6 46.8 %copy-start = (bf16[1024,1024]{1,0:T(8,128)(2,1)S(1)}, bf16[1024,1024]{1,0:T(8,128)(2,1)}, u32[]{:S(2)}) copy-start(bf16[1024,1024]{1,0:T(8,128)(2,1)} %param.7) | copy-start | bytes 6291460
  0.6 8.0 %collective-permute-start = (bf16[8,1024]{1,0:T(8,128)(2,1)}, bf16[8,1024]{1,0:T(8,128)(2,1)S(1)}, u32[]{:S(2)}, u32[]{:S(2)}) collective-permute-start(bf16[8,1024]{1,0:T(8,128)(2,1)} %param.6), channel_id=1, source_target_pairs={{0,4},{4,8},{8,12},{12,16},{16,20},{20,24},{24,28},{28,0},{1,5},{5... | collective-permute-start | bytes 49160 | tf_op jit(solution)/shard_map/ppermute | solution.py:27
  8.6 6.4 %collective-permute-start.1 = (bf16[8,1024]{1,0:T(8,128)(2,1)S(1)}, bf16[8,1024]{1,0:T(8,128)(2,1)S(1)}, u32[]{:S(2)}, u32[]{:S(2)}) collective-permute-start(bf16[8,1024]{1,0:T(8,128)(2,1)S(1)} %collective-permute-done), channel_id=1, source_target_pairs={{0,4},{4,8},{8,12},{12,16},{16,20},{20,24},{24,28},{28,0},{1,5},{5... | collective-permute-start | bytes 49160 | tf_op jit(solution)/shard_map/ppermute | solution.py:27
  15.1 6.4 %collective-permute-start.2 = (bf16[8,1024]{1,0:T(8,128)(2,1)S(1)}, bf16[8,1024]{1,0:T(8,128)(2,1)S(1)}, u32[]{:S(2)}, u32[]{:S(2)}) collective-permute-start(bf16[8,1024]{1,0:T(8,128)(2,1)S(1)} %collective-permute-done.1), channel_id=1, source_target_pairs={{0,4},{4,8},{8,12},{12,16},{16,20},{20,24},{24,28},{28,0},{1,5},{5... | collective-permute-start | bytes 49160 | tf_op jit(solution)/shard_map/ppermute | solution.py:27
  21.5 6.4 %collective-permute-start.3 = (bf16[8,1024]{1,0:T(8,128)(2,1)S(1)}, bf16[8,1024]{1,0:T(8,128)(2,1)S(1)}, u32[]{:S(2)}, u32[]{:S(2)}) collective-permute-start(bf16[8,1024]{1,0:T(8,128)(2,1)S(1)} %collective-permute-done.2), channel_id=1, source_target_pairs={{0,4},{4,8},{8,12},{12,16},{16,20},{20,24},{24,28},{28,0},{1,5},{5... | collective-permute-start | bytes 49160 | tf_op jit(solution)/shard_map/ppermute | solution.py:27
  27.9 6.5 %collective-permute-start.4 = (bf16[8,1024]{1,0:T(8,128)(2,1)S(1)}, bf16[8,1024]{1,0:T(8,128)(2,1)S(1)}, u32[]{:S(2)}, u32[]{:S(2)}) collective-permute-start(bf16[8,1024]{1,0:T(8,128)(2,1)S(1)} %collective-permute-done.3), channel_id=1, source_target_pairs={{0,4},{4,8},{8,12},{12,16},{16,20},{20,24},{24,28},{28,0},{1,5},{5... | collective-permute-start | bytes 49160 | tf_op jit(solution)/shard_map/ppermute | solution.py:27
  34.5 6.4 %collective-permute-start.5 = (bf16[8,1024]{1,0:T(8,128)(2,1)S(1)}, bf16[8,1024]{1,0:T(8,128)(2,1)S(1)}, u32[]{:S(2)}, u32[]{:S(2)}) collective-permute-start(bf16[8,1024]{1,0:T(8,128)(2,1)S(1)} %collective-permute-done.4), channel_id=1, source_target_pairs={{0,4},{4,8},{8,12},{12,16},{16,20},{20,24},{24,28},{28,0},{1,5},{5... | collective-permute-start | bytes 49160 | tf_op jit(solution)/shard_map/ppermute | solution.py:27
  40.9 6.4 %collective-permute-start.6 = (bf16[8,1024]{1,0:T(8,128)(2,1)S(1)}, bf16[8,1024]{1,0:T(8,128)(2,1)S(1)}, u32[]{:S(2)}, u32[]{:S(2)}) collective-permute-start(bf16[8,1024]{1,0:T(8,128)(2,1)S(1)} %collective-permute-done.5), channel_id=1, source_target_pairs={{0,4},{4,8},{8,12},{12,16},{16,20},{20,24},{24,28},{28,0},{1,5},{5... | collective-permute-start | bytes 49160 | tf_op jit(solution)/shard_map/ppermute | solution.py:27
  85.7 12.2 %all-to-all-start = ((bf16[64,4,256]{2,0,1:T(8,128)(2,1)}), bf16[64,4,256]{2,0,1:T(8,128)(2,1)S(1)}, u32[]{:S(2)}, u32[]{:S(2)}) async-start(bf16[64,4,256]{2,0,1:T(8,128)(2,1)} %bitcast.32), calls=%async_computation | async-start | bytes 262144 | tf_op jit(solution)/shard_map/all_to_all | solution.py:77
